TPU v7x, 32 devices: a whole 2x2x4 slice. The times are simulated.
32 devices in a mesh: tm: 2 (over y), pairs: 16 (over z, x, core).
Axes of the slice: x: 2, y: 2, z: 4, core: 2. Of those that a mesh axis runs over, the one named last changes fastest.
Arguments:
- records: bfloat16 [2, 512, 128, 2048], P('tm', 'pairs')
- source_map: int32 [2, 512], P('tm'), may hold values from 0 to 511, each once within a row
- pair_blocks: int32 [16, 6, 2], P('pairs'), may hold values from -1 to 31, as said below
Outputs:
- stacks: float32 [96, 16, 2, 128, 128], P('pairs', 'tm')
Inputs may be any that keep to these rules, and one draw needn't show every extreme that they name: `pair_blocks`: each pair slot holds blocks i <= j with j - i <= 2, or -1 and -1 when empty; every such pair appears in exactly one slot; some owner has all 6 slots filled. `source_map`: each row is a permutation: every slot of a time group holds exactly one window of one channel block.
All inputs are finite; a program needn't handle non-finite values.
Results may differ from a plain program's by a relative error of at most 0.0056.
Values may be sent and summed in bfloat16 or wider, within the bound.
A program may use at most 128 MiB of HBM per device.

v0:
```python
import math
import jax
import jax.numpy as jnp
from jax import lax
from jax.sharding import PartitionSpec as P

NB = 32
BINS = 16
FIRST_BIN = 64
WIN = 16


def transform_table(length):
    samples = jnp.arange(length, dtype=jnp.int32)
    bin_index = FIRST_BIN + jnp.arange(BINS, dtype=jnp.int32)
    phases = samples[:, None] * bin_index[None, :] % length
    angles = 2.0 * math.pi / length * phases.astype(jnp.float32)
    taper = 0.5 - 0.5 * jnp.cos(2.0 * math.pi / length * samples.astype(jnp.float32))
    weight_col = (taper / math.sqrt(length))[:, None]
    return jnp.concatenate(
        [jnp.cos(angles) * weight_col, -jnp.sin(angles) * weight_col], axis=1
    ).astype(jnp.bfloat16)


def whiten_spectra(windows, table):
    transformed = jnp.einsum("scn,nk->skc", windows, table, preferred_element_type=jnp.float32)
    real_part = transformed[:, :BINS]
    imag_part = transformed[:, BINS:]
    power = jnp.mean(real_part * real_part + imag_part * imag_part, axis=2, keepdims=True)
    inverse = 1.0 / jnp.sqrt(power + 1e-06)
    return (transformed * jnp.concatenate([inverse, inverse], axis=1)).astype(jnp.bfloat16)


def cross_stack(left_spec, right_spec):
    real_sum = jnp.einsum(
        "pwfi,pwfj->pfij",
        left_spec[:, :, 0],
        right_spec[:, :, 0],
        preferred_element_type=jnp.float32,
    )
    real_sum = real_sum + jnp.einsum(
        "pwfi,pwfj->pfij",
        left_spec[:, :, 1],
        right_spec[:, :, 1],
        preferred_element_type=jnp.float32,
    )
    imag_sum = jnp.einsum(
        "pwfi,pwfj->pfij",
        left_spec[:, :, 1],
        right_spec[:, :, 0],
        preferred_element_type=jnp.float32,
    )
    imag_sum = imag_sum - jnp.einsum(
        "pwfi,pwfj->pfij",
        left_spec[:, :, 0],
        right_spec[:, :, 1],
        preferred_element_type=jnp.float32,
    )
    return jnp.stack([real_sum, imag_sum], axis=2)


def per_device(records, source_map, pair_blocks):
    table = transform_table(records.shape[3])
    local_spec = whiten_spectra(records[0], table)
    channels = local_spec.shape[2]
    blocks = pair_blocks[0]
    slot_count = blocks.shape[0]
    valid = (blocks[:, 0] >= 0).astype(jnp.float32)
    safe_blocks = jnp.maximum(blocks, 0)
    window_ids = jnp.arange(WIN, dtype=jnp.int32)
    columns = window_ids[None, None, :] * NB + safe_blocks[:, :, None]
    wanted = jnp.take(source_map[0], columns.reshape(-1))
    piece = lax.all_gather(local_spec, "pairs", axis=0, tiled=True)
    row_ids = jnp.arange(piece.shape[0], dtype=jnp.int32)
    onehot = (wanted[:, None] == row_ids[None, :]).astype(jnp.bfloat16)
    collected = jnp.einsum("nr,rkc->nkc", onehot, piece, preferred_element_type=jnp.float32)
    picked = collected.astype(jnp.bfloat16)
    chosen = picked.reshape(slot_count, 2, WIN, 2, BINS, channels)
    norm_factor = 1.0 / math.sqrt(WIN * lax.axis_size("tm"))
    partial_stack = cross_stack(chosen[:, 0], chosen[:, 1])
    summed = lax.psum_scatter(partial_stack, "tm", scatter_dimension=1, tiled=True)
    return summed * (valid * norm_factor)[:, None, None, None, None]


def solution(mesh):
    return jax.shard_map(
        per_device,
        mesh=mesh,
        in_specs=(P("tm", "pairs", None, None), P("tm", None), P("pairs", None, None)),
        out_specs=P("pairs", "tm", None, None, None),
        check_vma=False,
    )
```

profile of v0, /device:TPU:0, one launch (start us, length us, event | category | flops | bytes accessed | tf_op | source)
XLA Modules:
  0.0 275.5 jit_solution(10862450789281669629)
XLA Ops:
  6.5 0.0 all-gather.2.cloned.1.call-start
  6.5 0.1 subtract_multiply_fusion
  6.6 0.6 multiply_convert_fusion.2
  7.2 0.0 copy-start.2
  7.2 8.6 %fusion.7 = f32[32,32,128]{2,1,0:T(8,128)S(1)} fusion(bf16[1,32,128,2048]{3,2,1,0:T(8,128)(2,1)} %param.3, bf16[2048,16]{0,1:T(8,128)(2,1)S(1)} %get-tuple-element.8, bf16[2048,16]{0,1:T(8,128)(2,1)S(1)} %get-tuple-element.7), kind=kOutput, calls=%fused_computation.11 | convolution fusion | flops 537133056 | bytes 17432576 | tf_op jit(solution)/shard_map/scn,nk->skc/dot_general | solution.py:26
  15.8 0.2 fusion.15
  16.0 0.1 maximum_bitcast_fusion.2
  16.1 0.9 multiply_convert_fusion
  17.0 0.0 all-gather.2.cloned.1.call-update
  17.0 0.0 reduce-scatter.5.cloned.1.call-start
  17.1 0.1 copy.14
  17.2 0.1 broadcast_add_fusion
  17.2 0.1 add.102
  17.3 0.1 add.99
  17.4 1.8 gather_fusion
  19.2 51.1 %all-gather.2.cloned.1.call-done = bf16[512,32,128]{2,1,0:T(8,128)(2,1)} async-done(((bf16[32,32,128]{2,1,0:T(8,128)(2,1)}), bf16[512,32,128]{2,1,0:T(8,128)(2,1)}) %all-gather.2.cloned.1.call-update) | async-done | bytes 4194320 | tf_op jit(solution)/shard_map/all_gather | solution.py:73
  70.4 4.0 %fusion.4 = bf16[192,32,128]{2,0,1:T(8,128)(2,1)S(1)} fusion(bf16[512,32,128]{2,1,0:T(8,128)(2,1)} %all-gather.2.cloned.1.call-done, s32[192]{0:T(256)S(1)} %and_select_fusion), kind=kOutput, calls=%fused_computation.10 | convolution fusion | flops 806191104 | bytes 5767936 | tf_op jit(solution)/shard_map/nr,rkc->nkc/dot_general | solution.py:76
  74.4 0.3 fusion.27
  74.7 0.4 copy_bitcast_fusion.1
  75.1 1.0 fusion.12
  76.1 1.0 fusion.13
  77.1 1.0 add_bitcast_fusion
  78.2 3.7 %subtract_bitcast_fusion = f32[6,16,1,128,128]{4,3,1,0,2:T(8,128)} fusion(f32[6,16,128,128]{3,2,1,0:T(8,128)S(1)} %fusion.13, bf16[6,16,2,16,128]{4,1,3,0,2:T(8,128)(2,1)S(1)} %get-tuple-element.10, bf16[6,16,2,16,128]{4,1,3,0,2:T(8,128)(2,1)S(1)} %get-tuple-element.9), kind=kOutput, calls=%fused_computation.6 | convolution fusion | flops 51904512 | bytes 13369344 | tf_op jit(solution)/shard_map/pwfi,pwfj->pfij/dot_general | solution.py:53
  81.9 9.6 %pad_maximum_fusion = f32[6,16,2,128,128]{4,3,1,0,2:T(8,128)} fusion(f32[6,16,1,128,128]{4,3,1,0,2:T(8,128)} %subtract_bitcast_fusion, f32[6,16,1,128,128]{4,3,1,0,2:T(8,128)S(1)} %add_bitcast_fusion), kind=kLoop, calls=%fused_computation.4 | loop fusion | flops 3145728 | bytes 25165824 | tf_op jit(solution)/shard_map/stack | solution.py:59
  91.5 11.3 %copy.19 = f32[6,16,2,128,128]{4,3,0,2,1:T(8,128)} copy(f32[6,16,2,128,128]{4,3,1,0,2:T(8,128)} %pad_maximum_fusion) | data formatting | bytes 25165824
  102.8 14.4 %copy.33 = f32[2,8,1536,128]{3,1,2,0:T(8,128)} copy(f32[2,8,1536,128]{3,2,1,0:T(8,128)} %bitcast.64) | data formatting | bytes 25165824
  117.2 0.0 reduce-scatter.5.cloned.1.call-update
  117.2 143.1 %reduce-scatter.5.cloned.1.call-done = f32[8,196608]{1,0:T(8,128)} async-done(((f32[16,196608]{1,0:T(8,128)}), f32[8,196608]{1,0:T(8,128)}) %reduce-scatter.5.cloned.1.call-update) | async-done | bytes 6291472
  260.4 4.0 %copy.24 = f32[1,8,1536,128]{3,2,1,0:T(8,128)S(1)} copy(f32[1,8,1536,128]{3,1,2,0:T(8,128)} %bitcast.66) | data formatting | bytes 12582912
  264.4 0.0 copy-start.1
  264.4 1.1 copy_multiply_fusion
  265.5 3.1 %copy.18 = f32[6,8,2,128,128]{4,3,2,1,0:T(8,128)} copy(f32[6,8,2,128,128]{4,3,1,0,2:T(8,128)S(1)} %copy_multiply_fusion) | data formatting | bytes 12582912 | tf_op jit(solution)/shard_map/mul | solution.py:82
  (12 shorter events, 0.0 us)
Async XLA Ops:
  6.5 10.9 %copy-start = (s32[1,512]{1,0:T(1,128)S(1)}, s32[1,512]{1,0:T(1,128)}, u32[]{:S(2)}) copy-start(s32[1,512]{1,0:T(1,128)} %param.4) | copy-start | bytes 6148
  6.5 63.9 %all-gather.2.cloned.1.call-start = ((), (), s32[]{:S(2)}) async-start(), calls=%async_computation.1 | async-start | bytes 4456448 | tf_op jit(solution)/shard_map/all_gather | solution.py:73
  7.2 9.8 %copy-start.2 = (s32[1,6,2]{1,2,0:T(2,128)S(1)}, s32[1,6,2]{1,2,0:T(2,128)}, u32[]{:S(2)}) copy-start(s32[1,6,2]{1,2,0:T(2,128)} %param.5) | copy-start | bytes 148
  17.0 243.4 %reduce-scatter.5.cloned.1.call-start = ((), (), s32[]{:S(2)}) async-start(), calls=%async_computation.2 | async-start | bytes 18874368
  264.4 4.3 %copy-start.1 = (s32[1,512]{1,0:T(1,128)S(1)}, s32[1,512]{1,0:T(1,128)}, u32[]{:S(2)}) copy-start(s32[1,512]{1,0:T(1,128)} %param.4) | copy-start | bytes 6148
Sparse Core Ops, SparseCore 0:
  17.1 53.2 all-gather.1
  117.3 142.9 reduce-scatter.4
where the time goes:
time: 276 us
  waiting for transfers between devices  194 us (70%)
  local copies, waits for them, and re-layouts  35.6 us (13%)
  matrix products  19.3 us (7%)
  between operations  13.6 us (5%)
  other arithmetic  12.7 us (5%)
    unnamed x3, waiting for transfers between devices  143 us
    all_gather x1, waiting for transfers between devices, per_device(): piece = lax.all_gather(local_spec, 'pairs', axis=0, tiled=True)  51.1 us
    unnamed x9, local copies, waits for them, and re-layouts  29.7 us
    another operation x1, other arithmetic, cross_stack(): return jnp.stack([real_sum, imag_sum], axis=2)  9.6 us
    dot_general x1, matrix products, whiten_spectra(): jnp.einsum('scn,nk->skc', windows, table, preferred_element_type=jnp.floa...  8.57 us
  transfers between devices with their start and end apart: 2, of which 2 were waited for; matrix products, arithmetic and copies ran while one was open for 1% of the time, Pallas kernels for 0%

commit v1 on v0

--- a/solution.py
+++ b/solution.py
@@ -3,6 +3,7 @@
 import jax.numpy as jnp
 from jax import lax
 from jax.sharding import PartitionSpec as P
+from jax.lax import axis_index, axis_size, ppermute
 
 NB = 32
 BINS = 16
@@ -70,7 +71,19 @@
     window_ids = jnp.arange(WIN, dtype=jnp.int32)
     columns = window_ids[None, None, :] * NB + safe_blocks[:, :, None]
     wanted = jnp.take(source_map[0], columns.reshape(-1))
-    piece = lax.all_gather(local_spec, "pairs", axis=0, tiled=True)
+    num = axis_size("pairs")
+    kept_rows = [(h, (h + 1) % num) for h in range(num)]
+    parts_seen = [(h, (h - 1) % num) for h in range(num)]
+    n_now, z = ([local_spec], [local_spec])
+    for _ in range(num // 2):
+        n_now.append(ppermute(n_now[-1], axis_name="pairs", perm=kept_rows))
+    it = 0
+    while it < (num - 1) // 2:
+        block_last = ppermute(z[-1], axis_name="pairs", perm=parts_seen)
+        z.append(block_last)
+        it = it + 1
+    newest = jnp.concatenate([*n_now[::-1], *z[1:]], axis=0)
+    piece = jnp.roll(newest, (axis_index("pairs") - num // 2) * local_spec.shape[0], axis=0)
     row_ids = jnp.arange(piece.shape[0], dtype=jnp.int32)
     onehot = (wanted[:, None] == row_ids[None, :]).astype(jnp.bfloat16)
     collected = jnp.einsum("nr,rkc->nkc", onehot, piece, preferred_element_type=jnp.float32)

time: 276 us -> 299 us (1.083)
  starting transfers between devices: 0.04 us -> 32.2 us
  waiting for transfers between devices: 194 us -> 180 us
  local copies, waits for them, and re-layouts: 35.6 us -> 42.9 us
    all_gather x1 -> x0, waiting for transfers between devices: 51.1 us -> none  [per_device(): piece = lax.all_gather(local_spec, 'pairs', axis=0, tiled=True)]
    ppermute x0 -> x15, waiting for transfers between devices: none -> 36 us  [the longest x8 36 us: per_device(): n_now.append(ppermute(n_now[-1], axis_name='pairs', perm=kept_rows))]
    ppermute x0 -> x15, starting transfers between devices: none -> 32.2 us  [the longest x7 31.6 us: per_device(): block_last = ppermute(z[-1], axis_name='pairs', perm=parts_seen)]
    unnamed x9 -> x38, local copies, waits for them, and re-layouts: 29.7 us -> 36.4 us
    unnamed x3 -> x2, waiting for transfers between devices: 143 us -> 144 us
  transfers between devices with their start and end apart: 2 -> 16, of which waited for: 2 -> 9; matrix products, arithmetic and copies ran while one was open for 1% -> 2% of each run, Pallas kernels for 0% -> 0%
where the time goes in v1:
time: 299 us
  waiting for transfers between devices  180 us (60%)
  local copies, waits for them, and re-layouts  42.9 us (14%)
  starting transfers between devices  32.2 us (11%)
  matrix products  17.2 us (6%)
  between operations  13.8 us (5%)
  other arithmetic  12.5 us (4%)
    unnamed x2, waiting for transfers between devices  144 us
    unnamed x38, local copies, waits for them, and re-layouts  36.4 us
    ppermute x8, waiting for transfers between devices, per_device(): n_now.append(ppermute(n_now[-1], axis_name='pairs', perm=kept_rows))  36 us
    ppermute x7, starting transfers between devices, per_device(): block_last = ppermute(z[-1], axis_name='pairs', perm=parts_seen)  31.6 us
    another operation x1, other arithmetic, cross_stack(): return jnp.stack([real_sum, imag_sum], axis=2)  9.62 us
    dot_general x1, matrix products, whiten_spectra(): jnp.einsum('scn,nk->skc', windows, table, preferred_element_type=jnp.floa...  8.57 us
  transfers between devices with their start and end apart: 16, of which 9 were waited for; matrix products, arithmetic and copies ran while one was open for 2% of the time, Pallas kernels for 0%

profile of v1, /device:TPU:0, one launch (start us, length us, event | category | flops | bytes accessed | tf_op | source)
XLA Modules:
  0.0 299.0 jit_solution(6664186120410779246)
XLA Ops:
  7.2 8.6 %fusion.7 = f32[32,32,128]{2,1,0:T(8,128)S(1)} fusion(bf16[1,32,128,2048]{3,2,1,0:T(8,128)(2,1)} %param.3, bf16[2048,16]{0,1:T(8,128)(2,1)S(1)} %get-tuple-element.8, bf16[2048,16]{0,1:T(8,128)(2,1)S(1)} %get-tuple-element.7), kind=kOutput, calls=%fused_computation.11 | convolution fusion | flops 537133056 | bytes 17432576 | tf_op jit(solution)/shard_map/scn,nk->skc/dot_general | solution.py:27
  16.8 9.0 %collective-permute-done = bf16[32,32,128]{2,1,0:T(8,128)(2,1)S(1)} collective-permute-done((bf16[32,32,128]{2,1,0:T(8,128)(2,1)S(1)}, bf16[32,32,128]{2,1,0:T(8,128)(2,1)S(1)}, u32[]{:S(2)}, u32[]{:S(2)}) %collective-permute-start) | collective-permute-done | bytes 262176 | tf_op jit(solution)/shard_map/ppermute | solution.py:79
  25.8 4.4 %collective-permute-start.8 = (bf16[32,32,128]{2,1,0:T(8,128)(2,1)S(1)}, bf16[32,32,128]{2,1,0:T(8,128)(2,1)S(1)}, u32[]{:S(2)}, u32[]{:S(2)}) collective-permute-start(bf16[32,32,128]{2,1,0:T(8,128)(2,1)S(1)} %multiply_convert_fusion), channel_id=1, source_target_pairs={{0,15},{1,0},{2,1},{3,2},{4,3},{5,4},{6,5},{7,6},{8,7},{9,8},{10,9... | collective-permute-start | bytes 786440 | tf_op jit(solution)/shard_map/ppermute | solution.py:82
  30.2 4.1 %collective-permute-done.1 = bf16[32,32,128]{2,1,0:T(8,128)(2,1)S(1)} collective-permute-done((bf16[32,32,128]{2,1,0:T(8,128)(2,1)S(1)}, bf16[32,32,128]{2,1,0:T(8,128)(2,1)S(1)}, u32[]{:S(2)}, u32[]{:S(2)}) %collective-permute-start.1) | collective-permute-done | bytes 262176 | tf_op jit(solution)/shard_map/ppermute | solution.py:79
  34.3 4.5 %collective-permute-start.9 = (bf16[32,32,128]{2,1,0:T(8,128)(2,1)S(1)}, bf16[32,32,128]{2,1,0:T(8,128)(2,1)S(1)}, u32[]{:S(2)}, u32[]{:S(2)}) collective-permute-start(bf16[32,32,128]{2,1,0:T(8,128)(2,1)S(1)} %collective-permute-done.8), channel_id=1, source_target_pairs={{0,15},{1,0},{2,1},{3,2},{4,3},{5,4},{6,5},{7,6},{8,7},{9,8},{10,9... | collective-permute-start | bytes 786440 | tf_op jit(solution)/shard_map/ppermute | solution.py:82
  38.8 4.1 %collective-permute-done.2 = bf16[32,32,128]{2,1,0:T(8,128)(2,1)S(1)} collective-permute-done((bf16[32,32,128]{2,1,0:T(8,128)(2,1)S(1)}, bf16[32,32,128]{2,1,0:T(8,128)(2,1)S(1)}, u32[]{:S(2)}, u32[]{:S(2)}) %collective-permute-start.2) | collective-permute-done | bytes 262176 | tf_op jit(solution)/shard_map/ppermute | solution.py:79
  42.9 4.5 %collective-permute-start.10 = (bf16[32,32,128]{2,1,0:T(8,128)(2,1)S(1)}, bf16[32,32,128]{2,1,0:T(8,128)(2,1)S(1)}, u32[]{:S(2)}, u32[]{:S(2)}) collective-permute-start(bf16[32,32,128]{2,1,0:T(8,128)(2,1)S(1)} %collective-permute-done.9), channel_id=1, source_target_pairs={{0,15},{1,0},{2,1},{3,2},{4,3},{5,4},{6,5},{7,6},{8,7},{9,8},{10,9... | collective-permute-start | bytes 786440 | tf_op jit(solution)/shard_map/ppermute | solution.py:82
  47.4 4.1 %collective-permute-done.3 = bf16[32,32,128]{2,1,0:T(8,128)(2,1)S(1)} collective-permute-done((bf16[32,32,128]{2,1,0:T(8,128)(2,1)S(1)}, bf16[32,32,128]{2,1,0:T(8,128)(2,1)S(1)}, u32[]{:S(2)}, u32[]{:S(2)}) %collective-permute-start.3) | collective-permute-done | bytes 262176 | tf_op jit(solution)/shard_map/ppermute | solution.py:79
  51.5 4.5 %collective-permute-start.11 = (bf16[32,32,128]{2,1,0:T(8,128)(2,1)S(1)}, bf16[32,32,128]{2,1,0:T(8,128)(2,1)S(1)}, u32[]{:S(2)}, u32[]{:S(2)}) collective-permute-start(bf16[32,32,128]{2,1,0:T(8,128)(2,1)S(1)} %collective-permute-done.10), channel_id=1, source_target_pairs={{0,15},{1,0},{2,1},{3,2},{4,3},{5,4},{6,5},{7,6},{8,7},{9,8},{10,9... | collective-permute-start | bytes 786440 | tf_op jit(solution)/shard_map/ppermute | solution.py:82
  56.0 4.1 %collective-permute-done.4 = bf16[32,32,128]{2,1,0:T(8,128)(2,1)S(1)} collective-permute-done((bf16[32,32,128]{2,1,0:T(8,128)(2,1)S(1)}, bf16[32,32,128]{2,1,0:T(8,128)(2,1)S(1)}, u32[]{:S(2)}, u32[]{:S(2)}) %collective-permute-start.4) | collective-permute-done | bytes 262176 | tf_op jit(solution)/shard_map/ppermute | solution.py:79
  60.2 4.5 %collective-permute-start.12 = (bf16[32,32,128]{2,1,0:T(8,128)(2,1)S(1)}, bf16[32,32,128]{2,1,0:T(8,128)(2,1)S(1)}, u32[]{:S(2)}, u32[]{:S(2)}) collective-permute-start(bf16[32,32,128]{2,1,0:T(8,128)(2,1)S(1)} %collective-permute-done.11), channel_id=1, source_target_pairs={{0,15},{1,0},{2,1},{3,2},{4,3},{5,4},{6,5},{7,6},{8,7},{9,8},{10,9... | collective-permute-start | bytes 786440 | tf_op jit(solution)/shard_map/ppermute | solution.py:82
  64.7 4.1 %collective-permute-done.5 = bf16[32,32,128]{2,1,0:T(8,128)(2,1)} collective-permute-done((bf16[32,32,128]{2,1,0:T(8,128)(2,1)S(1)}, bf16[32,32,128]{2,1,0:T(8,128)(2,1)}, u32[]{:S(2)}, u32[]{:S(2)}) %collective-permute-start.5) | collective-permute-done | bytes 262176 | tf_op jit(solution)/shard_map/ppermute | solution.py:79
  69.0 4.5 %collective-permute-start.13 = (bf16[32,32,128]{2,1,0:T(8,128)(2,1)S(1)}, bf16[32,32,128]{2,1,0:T(8,128)(2,1)S(1)}, u32[]{:S(2)}, u32[]{:S(2)}) collective-permute-start(bf16[32,32,128]{2,1,0:T(8,128)(2,1)S(1)} %collective-permute-done.12), channel_id=1, source_target_pairs={{0,15},{1,0},{2,1},{3,2},{4,3},{5,4},{6,5},{7,6},{8,7},{9,8},{10,9... | collective-permute-start | bytes 786440 | tf_op jit(solution)/shard_map/ppermute | solution.py:82
  73.5 4.2 %collective-permute-done.6 = bf16[32,32,128]{2,1,0:T(8,128)(2,1)} collective-permute-done((bf16[32,32,128]{2,1,0:T(8,128)(2,1)}, bf16[32,32,128]{2,1,0:T(8,128)(2,1)}, u32[]{:S(2)}, u32[]{:S(2)}) %collective-permute-start.6) | collective-permute-done | bytes 262176 | tf_op jit(solution)/shard_map/ppermute | solution.py:79
  77.8 1.6 gather_fusion
  79.5 4.7 %collective-permute-start.14 = (bf16[32,32,128]{2,1,0:T(8,128)(2,1)S(1)}, bf16[32,32,128]{2,1,0:T(8,128)(2,1)S(1)}, u32[]{:S(2)}, u32[]{:S(2)}) collective-permute-start(bf16[32,32,128]{2,1,0:T(8,128)(2,1)S(1)} %collective-permute-done.13), channel_id=1, source_target_pairs={{0,15},{1,0},{2,1},{3,2},{4,3},{5,4},{6,5},{7,6},{8,7},{9,8},{10,9... | collective-permute-start | bytes 786440 | tf_op jit(solution)/shard_map/ppermute | solution.py:82
  84.1 2.4 collective-permute-done.7
  87.5 1.0 constant_dynamic-update-slice_fusion.30
  88.5 1.0 constant_dynamic-update-slice_fusion.29
  90.3 1.0 constant_dynamic-update-slice_fusion.15
  94.8 1.9 fusion.4
  97.4 1.0 fusion.12
  98.4 1.0 fusion.13
  99.4 1.0 add_bitcast_fusion
  100.5 3.7 %subtract_bitcast_fusion = f32[6,16,1,128,128]{4,3,1,0,2:T(8,128)} fusion(f32[6,16,128,128]{3,2,1,0:T(8,128)S(1)} %fusion.13, bf16[6,16,2,16,128]{4,1,3,0,2:T(8,128)(2,1)S(1)} %get-tuple-element.10, bf16[6,16,2,16,128]{4,1,3,0,2:T(8,128)(2,1)S(1)} %get-tuple-element.9), kind=kOutput, calls=%fused_computation.6 | convolution fusion | flops 51904512 | bytes 13369344 | tf_op jit(solution)/shard_map/pwfi,pwfj->pfij/dot_general | solution.py:54
  104.2 9.6 %pad_maximum_fusion = f32[6,16,2,128,128]{4,3,1,0,2:T(8,128)} fusion(f32[6,16,1,128,128]{4,3,1,0,2:T(8,128)} %subtract_bitcast_fusion, f32[6,16,1,128,128]{4,3,1,0,2:T(8,128)S(1)} %add_bitcast_fusion), kind=kLoop, calls=%fused_computation.4 | loop fusion | flops 3145728 | bytes 25165824 | tf_op jit(solution)/shard_map/stack | solution.py:60
  113.8 11.3 %copy.19 = f32[6,16,2,128,128]{4,3,0,2,1:T(8,128)} copy(f32[6,16,2,128,128]{4,3,1,0,2:T(8,128)} %pad_maximum_fusion) | data formatting | bytes 25165824
  125.1 14.4 %copy.33 = f32[2,8,1536,128]{3,1,2,0:T(8,128)} copy(f32[2,8,1536,128]{3,2,1,0:T(8,128)} %bitcast.64) | data formatting | bytes 25165824
  139.5 144.3 %reduce-scatter.5.cloned.1.call-done = f32[8,196608]{1,0:T(8,128)} async-done(((f32[16,196608]{1,0:T(8,128)}), f32[8,196608]{1,0:T(8,128)}) %reduce-scatter.5.cloned.1.call-update) | async-done | bytes 6291472
  283.8 4.0 %copy.24 = f32[1,8,1536,128]{3,2,1,0:T(8,128)S(1)} copy(f32[1,8,1536,128]{3,1,2,0:T(8,128)} %bitcast.66) | data formatting | bytes 12582912
  287.8 1.1 copy_multiply_fusion
  289.0 3.1 %copy.18 = f32[6,8,2,128,128]{4,3,2,1,0:T(8,128)} copy(f32[6,8,2,128,128]{4,3,1,0,2:T(8,128)S(1)} %copy_multiply_fusion) | data formatting | bytes 12582912 | tf_op jit(solution)/shard_map/mul | solution.py:95
  (72 shorter events, 7.8 us)
Async XLA Ops:
  6.5 71.3 %copy-start = (s32[1,512]{1,0:T(1,128)S(1)}, s32[1,512]{1,0:T(1,128)}, u32[]{:S(2)}) copy-start(s32[1,512]{1,0:T(1,128)} %param.4) | copy-start | bytes 6148
  6.5 277.3 %reduce-scatter.5.cloned.1.call-start = ((), (), s32[]{:S(2)}) async-start(), calls=%async_computation.1 | async-start | bytes 18874368
  7.2 52.9 %copy-start.2 = (s32[1,6,2]{1,2,0:T(2,128)S(1)}, s32[1,6,2]{1,2,0:T(2,128)}, u32[]{:S(2)}) copy-start(s32[1,6,2]{1,2,0:T(2,128)} %param.5) | copy-start | bytes 148
  16.3 9.5 %collective-permute-start = (bf16[32,32,128]{2,1,0:T(8,128)(2,1)S(1)}, bf16[32,32,128]{2,1,0:T(8,128)(2,1)S(1)}, u32[]{:S(2)}, u32[]{:S(2)}) collective-permute-start(bf16[32,32,128]{2,1,0:T(8,128)(2,1)S(1)} %multiply_convert_fusion), channel_id=1, source_target_pairs={{0,1},{1,2},{2,3},{3,4},{4,5},{5,6},{6,7},{7,8},{8,9},{9,10},{10,1... | collective-permute-start | bytes 786440 | tf_op jit(solution)/shard_map/ppermute | solution.py:79
  25.8 8.5 %collective-permute-start.1 = (bf16[32,32,128]{2,1,0:T(8,128)(2,1)S(1)}, bf16[32,32,128]{2,1,0:T(8,128)(2,1)S(1)}, u32[]{:S(2)}, u32[]{:S(2)}) collective-permute-start(bf16[32,32,128]{2,1,0:T(8,128)(2,1)S(1)} %collective-permute-done), channel_id=1, source_target_pairs={{0,1},{1,2},{2,3},{3,4},{4,5},{5,6},{6,7},{7,8},{8,9},{9,10},{10,1... | collective-permute-start | bytes 786440 | tf_op jit(solution)/shard_map/ppermute | solution.py:79
  25.8 8.5 %collective-permute-start.8 = (bf16[32,32,128]{2,1,0:T(8,128)(2,1)S(1)}, bf16[32,32,128]{2,1,0:T(8,128)(2,1)S(1)}, u32[]{:S(2)}, u32[]{:S(2)}) collective-permute-start(bf16[32,32,128]{2,1,0:T(8,128)(2,1)S(1)} %multiply_convert_fusion), channel_id=1, source_target_pairs={{0,15},{1,0},{2,1},{3,2},{4,3},{5,4},{6,5},{7,6},{8,7},{9,8},{10,9... | collective-permute-start | bytes 786440 | tf_op jit(solution)/shard_map/ppermute | solution.py:82
  34.3 8.6 %collective-permute-start.2 = (bf16[32,32,128]{2,1,0:T(8,128)(2,1)S(1)}, bf16[32,32,128]{2,1,0:T(8,128)(2,1)S(1)}, u32[]{:S(2)}, u32[]{:S(2)}) collective-permute-start(bf16[32,32,128]{2,1,0:T(8,128)(2,1)S(1)} %collective-permute-done.1), channel_id=1, source_target_pairs={{0,1},{1,2},{2,3},{3,4},{4,5},{5,6},{6,7},{7,8},{8,9},{9,10},{10,1... | collective-permute-start | bytes 786440 | tf_op jit(solution)/shard_map/ppermute | solution.py:79
  34.3 8.6 %collective-permute-start.9 = (bf16[32,32,128]{2,1,0:T(8,128)(2,1)S(1)}, bf16[32,32,128]{2,1,0:T(8,128)(2,1)S(1)}, u32[]{:S(2)}, u32[]{:S(2)}) collective-permute-start(bf16[32,32,128]{2,1,0:T(8,128)(2,1)S(1)} %collective-permute-done.8), channel_id=1, source_target_pairs={{0,15},{1,0},{2,1},{3,2},{4,3},{5,4},{6,5},{7,6},{8,7},{9,8},{10,9... | collective-permute-start | bytes 786440 | tf_op jit(solution)/shard_map/ppermute | solution.py:82
  42.9 8.6 %collective-permute-start.3 = (bf16[32,32,128]{2,1,0:T(8,128)(2,1)S(1)}, bf16[32,32,128]{2,1,0:T(8,128)(2,1)S(1)}, u32[]{:S(2)}, u32[]{:S(2)}) collective-permute-start(bf16[32,32,128]{2,1,0:T(8,128)(2,1)S(1)} %collective-permute-done.2), channel_id=1, source_target_pairs={{0,1},{1,2},{2,3},{3,4},{4,5},{5,6},{6,7},{7,8},{8,9},{9,10},{10,1... | collective-permute-start | bytes 786440 | tf_op jit(solution)/shard_map/ppermute | solution.py:79
  42.9 8.6 %collective-permute-start.10 = (bf16[32,32,128]{2,1,0:T(8,128)(2,1)S(1)}, bf16[32,32,128]{2,1,0:T(8,128)(2,1)S(1)}, u32[]{:S(2)}, u32[]{:S(2)}) collective-permute-start(bf16[32,32,128]{2,1,0:T(8,128)(2,1)S(1)} %collective-permute-done.9), channel_id=1, source_target_pairs={{0,15},{1,0},{2,1},{3,2},{4,3},{5,4},{6,5},{7,6},{8,7},{9,8},{10,9... | collective-permute-start | bytes 786440 | tf_op jit(solution)/shard_map/ppermute | solution.py:82
  51.5 8.6 %collective-permute-start.4 = (bf16[32,32,128]{2,1,0:T(8,128)(2,1)S(1)}, bf16[32,32,128]{2,1,0:T(8,128)(2,1)S(1)}, u32[]{:S(2)}, u32[]{:S(2)}) collective-permute-start(bf16[32,32,128]{2,1,0:T(8,128)(2,1)S(1)} %collective-permute-done.3), channel_id=1, source_target_pairs={{0,1},{1,2},{2,3},{3,4},{4,5},{5,6},{6,7},{7,8},{8,9},{9,10},{10,1... | collective-permute-start | bytes 786440 | tf_op jit(solution)/shard_map/ppermute | solution.py:79
  51.5 8.7 %collective-permute-start.11 = (bf16[32,32,128]{2,1,0:T(8,128)(2,1)S(1)}, bf16[32,32,128]{2,1,0:T(8,128)(2,1)S(1)}, u32[]{:S(2)}, u32[]{:S(2)}) collective-permute-start(bf16[32,32,128]{2,1,0:T(8,128)(2,1)S(1)} %collective-permute-done.10), channel_id=1, source_target_pairs={{0,15},{1,0},{2,1},{3,2},{4,3},{5,4},{6,5},{7,6},{8,7},{9,8},{10,9... | collective-permute-start | bytes 786440 | tf_op jit(solution)/shard_map/ppermute | solution.py:82
  60.1 8.7 %collective-permute-start.5 = (bf16[32,32,128]{2,1,0:T(8,128)(2,1)S(1)}, bf16[32,32,128]{2,1,0:T(8,128)(2,1)}, u32[]{:S(2)}, u32[]{:S(2)}) collective-permute-start(bf16[32,32,128]{2,1,0:T(8,128)(2,1)S(1)} %collective-permute-done.4), channel_id=1, source_target_pairs={{0,1},{1,2},{2,3},{3,4},{4,5},{5,6},{6,7},{7,8},{8,9},{9,10},{10,1... | collective-permute-start | bytes 786440 | tf_op jit(solution)/shard_map/ppermute | solution.py:79
  60.2 8.8 %collective-permute-start.12 = (bf16[32,32,128]{2,1,0:T(8,128)(2,1)S(1)}, bf16[32,32,128]{2,1,0:T(8,128)(2,1)S(1)}, u32[]{:S(2)}, u32[]{:S(2)}) collective-permute-start(bf16[32,32,128]{2,1,0:T(8,128)(2,1)S(1)} %collective-permute-done.11), channel_id=1, source_target_pairs={{0,15},{1,0},{2,1},{3,2},{4,3},{5,4},{6,5},{7,6},{8,7},{9,8},{10,9... | collective-permute-start | bytes 786440 | tf_op jit(solution)/shard_map/ppermute | solution.py:82
  68.8 8.9 %collective-permute-start.6 = (bf16[32,32,128]{2,1,0:T(8,128)(2,1)}, bf16[32,32,128]{2,1,0:T(8,128)(2,1)}, u32[]{:S(2)}, u32[]{:S(2)}) collective-permute-start(bf16[32,32,128]{2,1,0:T(8,128)(2,1)} %collective-permute-done.5), channel_id=1, source_target_pairs={{0,1},{1,2},{2,3},{3,4},{4,5},{5,6},{6,7},{7,8},{8,9},{9,10},{10,1... | collective-permute-start | bytes 786440 | tf_op jit(solution)/shard_map/ppermute | solution.py:79
  69.0 10.5 %collective-permute-start.13 = (bf16[32,32,128]{2,1,0:T(8,128)(2,1)S(1)}, bf16[32,32,128]{2,1,0:T(8,128)(2,1)S(1)}, u32[]{:S(2)}, u32[]{:S(2)}) collective-permute-start(bf16[32,32,128]{2,1,0:T(8,128)(2,1)S(1)} %collective-permute-done.12), channel_id=1, source_target_pairs={{0,15},{1,0},{2,1},{3,2},{4,3},{5,4},{6,5},{7,6},{8,7},{9,8},{10,9... | collective-permute-start | bytes 786440 | tf_op jit(solution)/shard_map/ppermute | solution.py:82
  77.7 8.8 %collective-permute-start.7 = (bf16[32,32,128]{2,1,0:T(8,128)(2,1)}, bf16[32,32,128]{2,1,0:T(8,128)(2,1)}, u32[]{:S(2)}, u32[]{:S(2)}) collective-permute-start(bf16[32,32,128]{2,1,0:T(8,128)(2,1)} %collective-permute-done.6), channel_id=1, source_target_pairs={{0,1},{1,2},{2,3},{3,4},{4,5},{5,6},{6,7},{7,8},{8,9},{9,10},{10,1... | collective-permute-start | bytes 786440 | tf_op jit(solution)/shard_map/ppermute | solution.py:79
  79.5 10.7 %collective-permute-start.14 = (bf16[32,32,128]{2,1,0:T(8,128)(2,1)S(1)}, bf16[32,32,128]{2,1,0:T(8,128)(2,1)S(1)}, u32[]{:S(2)}, u32[]{:S(2)}) collective-permute-start(bf16[32,32,128]{2,1,0:T(8,128)(2,1)S(1)} %collective-permute-done.13), channel_id=1, source_target_pairs={{0,15},{1,0},{2,1},{3,2},{4,3},{5,4},{6,5},{7,6},{8,7},{9,8},{10,9... | collective-permute-start | bytes 786440 | tf_op jit(solution)/shard_map/ppermute | solution.py:82
  287.8 4.3 %copy-start.1 = (s32[1,512]{1,0:T(1,128)S(1)}, s32[1,512]{1,0:T(1,128)}, u32[]{:S(2)}) copy-start(s32[1,512]{1,0:T(1,128)} %param.4) | copy-start | bytes 6148
Sparse Core Ops, SparseCore 0:
  139.6 144.1 reduce-scatter.4
